TPU v7x, 32 devices: a whole 2x2x4 slice. The times are simulated.
32 devices in a mesh: sec: 8 (over z, x), tile: 4 (over y, core).
Axes of the slice: x: 2, y: 2, z: 4, core: 2. Of those that a mesh axis runs over, the one named last changes fastest.
Arguments:
- displacement: float32 [2, 8, 1024, 2048], P(None, 'sec', 'tile'), may hold values from -6 to 6
- spring: float32 [8, 1024, 2048], P('sec', 'tile'), may hold values from 0.5 to 2
- stiff_table: float32 [8], replicated, may hold values from 0.25 to 2
- match_blocks: int32 [2, 8, 1024], P(None, 'sec', 'tile'), may hold values from 0 to 4095
- match_class: int32 [8, 1024], P('sec', 'tile'), may hold values from 0 to 7
Outputs:
- relaxed: float32 [2, 8, 1024, 2048], P(None, 'sec', 'tile')
All inputs are finite; a program needn't handle non-finite values.
Results may differ from a plain program's by a relative error of at most 0.000053.
Values sent between devices are 32-bit elements; how exact they have to be, the bound alone decides.
No kernel may reach another device: no remote copies, remote signals or barrier semaphores. Data moves between devices by JAX's collectives and lax.ppermute only.
A program may use at most 128 MiB of HBM per device.

v0:
```python
import functools
import math
import jax
import jax.numpy as jnp
from jax import lax
from jax.experimental import pallas as pl
from jax.experimental.pallas import tpu as pltpu
from jax.sharding import PartitionSpec as P

ITERS = 3
LOADS = 4
GROUP = 6
OWN_VMEM = 47
LANES = 128
SUB = 8

VM = pl.BlockSpec(memory_space=pltpu.VMEM)
SM = pl.BlockSpec(memory_space=pltpu.SMEM)
HBM = pl.BlockSpec(memory_space=pltpu.MemorySpace.HBM)


def f32(*shape):
    return jax.ShapeDtypeStruct(shape, jnp.float32)


def tile_row(block, chunks):
    bits, low = chunks.bit_length() - 1, SUB.bit_length() - 1
    row = block >> bits
    return ((row >> low) << (bits + low)) | ((block & (chunks - 1)) << low) | (row & (SUB - 1))


def pieces(x, count):
    out = []
    for _ in range(count):
        out.append(x.astype(jnp.bfloat16))
        x = x - out[-1].astype(jnp.float32)
    return out


def summed(same, x, count=2):
    out = None
    for piece in pieces(x, count):
        product = jnp.dot(same, piece, preferred_element_type=jnp.float32)
        out = product if out is None else out + product
    return out


def parity(axis):
    return lax.axis_index(axis) % 2


def columns(line):
    return jnp.concatenate(
        [
            jnp.broadcast_to(line[:, at : at + LANES], (LANES, LANES)).T
            for at in range(0, line.shape[1], LANES)
        ],
        axis=0,
    )


def each_slot(count, rows, body):
    def some(step, carry):
        for inner in range(16):
            slot = step * 16 + inner
            body(slot, rows(slot))
        return carry

    lax.fori_loop(0, count // 16, some, 0)


def into_smem(line, staged, scalars, sem):
    staged[...] = line
    copy = pltpu.make_async_copy(staged, scalars, sem)
    copy.start()
    return copy


def load_parts(source, target, sem, pieces_each):
    rows = source.shape[1] // pieces_each
    copies = []
    for part in range(source.shape[0]):
        for piece in range(pieces_each):
            at = pl.ds(piece * rows, rows)
            copies.append(
                pltpu.make_async_copy(
                    source.at[part, at, :], target.at[part, at, :], sem.at[part * pieces_each + piece]
                )
            )
    return copies


def coupling_of(classes, table, alive):
    out = jnp.zeros(classes.shape, jnp.float32)
    for level in range(table.shape[1]):
        out = jnp.where(classes == level, table[:, level : level + 1], out)
    return out * alive.astype(jnp.float32)


def own_kernel(chunks, packed, displacement, field, entry, staged, scalars, sem, load_sem):
    loads = load_parts(displacement, field, load_sem, LOADS)
    for copy in loads:
        copy.start()
    listed = into_smem(tile_row(packed[0], chunks), staged, scalars, sem)
    listed.wait()
    for part in range(2):
        for copy in loads[part * LOADS : (part + 1) * LOADS]:
            copy.wait()

        def take(slot, row):
            entry[part, pl.ds(slot, 1), :] = field[part, pl.ds(row, 1), :]

        each_slot(packed.shape[2], lambda j: scalars[0, j], take)


def first_kernel(chunks, table, packed, prev, field, own_entry, entry, stiff, rows, send_x, send_z, edges, staged, scalars, taken, sem):
    blocks = field.shape[1]
    matches = own_entry.shape[1]
    count = 2 * matches
    own_rows, prev_rows = tile_row(packed[0], chunks), tile_row(prev[1], chunks)
    listed = into_smem(prev_rows, staged, scalars, sem)
    even = parity("sec") == 0
    section = lax.axis_index("sec")
    stiff_own = columns(coupling_of(packed[2], table, section < lax.axis_size("sec") - 1))
    stiff_prev = columns(coupling_of(prev[2], table, section > 0))
    rows[:, :matches] = jnp.where(even, own_rows, prev_rows)
    rows[:, matches:] = jnp.where(even, prev_rows, own_rows)
    for part in range(2):
        for chunk in range(chunks):
            entry[part, pl.ds(count + chunk, 1), :] = field[part, pl.ds(chunk * SUB, 1), :]
            entry[part, pl.ds(count + chunks + chunk, 1), :] = field[
                part, pl.ds(blocks - SUB * chunks + chunk * SUB + SUB - 1, 1), :
            ]
    edges[...] = entry[:, count:, :]
    listed.wait()

    def take(slot, row):
        for part in range(2):
            taken[part, pl.ds(slot, 1), :] = field[part, pl.ds(row, 1), :]

    each_slot(matches, lambda j: scalars[0, j], take)

    def place(values, coupling, at, send):
        stiff[at : at + matches, :] = coupling
        for part in range(2):
            value = values[part]
            entry[part, at : at + matches, :] = value
            send[part] = value * coupling

    @pl.when(even)
    def _():
        place(own_entry, stiff_own, 0, send_x)
        place(taken, stiff_prev, matches, send_z)

    @pl.when(jnp.logical_not(even))
    def _():
        place(taken, stiff_prev, 0, send_x)
        place(own_entry, stiff_own, matches, send_z)


def relate(rows_line, stiff, picked, column, same, weight, factor, chunks, blocks):
    count = rows_line.shape[1]
    total = count + 2 * chunks
    last = blocks - SUB * chunks + SUB - 1
    column[:count, :] = columns(rows_line[...].astype(jnp.float32))
    edge = lax.broadcasted_iota(jnp.int32, (chunks, LANES), 0) * SUB
    column[count : count + chunks, :] = edge.astype(jnp.float32)
    column[count + chunks :, :] = (edge + last).astype(jnp.float32)
    place = lax.broadcasted_iota(jnp.int32, (1, LANES), 1)
    edge_line = jnp.where(place < chunks, place * SUB, (place - chunks) * SUB + last)
    edge_line = jnp.where(place < 2 * chunks, edge_line, -1).astype(jnp.float32)

    def band(step, carry):
        at = pl.ds(pl.multiple_of(step * 32, 32), 32)
        col = column[at, :]
        for piece in range(count // LANES):
            cut = slice(piece * LANES, (piece + 1) * LANES)
            equal = col == rows_line[:, cut].astype(jnp.float32)
            same[at, cut] = equal.astype(jnp.float32).astype(jnp.bfloat16)
        same[at, count:] = (col == edge_line).astype(jnp.float32).astype(jnp.bfloat16)
        return carry

    lax.fori_loop(0, total // 32, band, 0)
    spring_here = picked[...]
    inverse = 1.0 / (4.0 * spring_here + summed(same[:, :count], stiff[...], 3))
    weight[...] = 4.0 * spring_here * inverse
    factor[...] = 0.8 * inverse


def stencil(field, nearby, start, chunks, top=False, bottom=False):
    span = SUB * chunks
    lane = lax.broadcasted_iota(jnp.int32, (SUB, LANES), 1)
    sub = lax.broadcasted_iota(jnp.int32, (SUB, LANES), 0)
    for part in range(2):

        def at(offset):
            return field[part, pl.ds(start + offset, SUB), :]

        before = jnp.zeros((SUB, LANES), jnp.float32)
        here = at(0)
        for chunk in range(chunks):
            offset = chunk * SUB
            after = at(offset + SUB) if chunk < chunks - 1 else jnp.zeros((SUB, LANES), jnp.float32)
            if top:
                up = jnp.where(sub == 0, 0.0, pltpu.roll(here, 1, 0))
            else:
                up = jnp.where(sub == 0, at(offset - span + SUB - 1), at(offset - 1))
            if bottom:
                down = jnp.where(sub == SUB - 1, 0.0, pltpu.roll(here, SUB - 1, 0))
            else:
                down = jnp.where(sub == SUB - 1, at(offset + span - SUB + 1), at(offset + 1))
            left = pltpu.roll(jnp.where(lane == LANES - 1, before, here), 1, 1)
            right = pltpu.roll(jnp.where(lane == 0, after, here), LANES - 1, 1)
            nearby[part, pl.ds(start + offset, SUB), :] = 0.2 * (((up + down) + (left + right)) + here)
            before, here = here, after


def strips_all(chunks, field, nearby):
    blocks = field.shape[1]
    span = SUB * chunks
    strips = blocks // span
    stencil(field, nearby, 0, chunks, top=True)
    stencil(field, nearby, blocks - span, chunks, bottom=True)
    group = math.gcd(strips - 2, GROUP)

    def some(step, carry):
        for inner in range(group):
            stencil(field, nearby, pl.multiple_of((1 + step * group + inner) * span, SUB), chunks)
        return carry

    lax.fori_loop(0, (strips - 2) // group, some, 0)


def each_entry(chunks, rows, blocks, take):
    count = rows.shape[1]
    each_slot(count, lambda j: rows[0, j], take)
    for chunk in range(chunks):
        take(count + chunk, chunk * SUB)
        take(count + chunks + chunk, blocks - SUB * chunks + chunk * SUB + SUB - 1)


def halo_rows(got_a, got_b):
    tile, tiles = lax.axis_index("tile"), lax.axis_size("tile")
    chunks = got_a.shape[1] // 2
    odd = tile % 2 == 1
    has_above, has_below = tile > 0, tile < tiles - 1
    out = []
    for part in range(2):
        (a_top, a_bottom), (b_top, b_bottom) = (
            (got[part, :chunks, :], got[part, chunks:, :]) for got in (got_a, got_b)
        )
        above, below = jnp.where(odd, a_bottom, b_bottom), jnp.where(odd, b_top, a_top)
        out.append((jnp.where(has_above, 0.2 * above, 0.0), jnp.where(has_below, 0.2 * below, 0.0)))
    return out


def add_halo(field, halos, chunks):
    last = field.shape[1] - SUB * chunks + SUB - 1
    for part, (above, below) in enumerate(halos):
        for chunk in range(chunks):
            for start, halo in ((0, above), (last, below)):
                at = pl.ds(start + chunk * SUB, 1)
                field[part, at, :] = field[part, at, :] + halo[chunk : chunk + 1, :]


def start_kernel(chunks, rows, rows_line, stiff, spring, field, nearby, base, same, weight, factor, picked, column):
    strips_all(chunks, field, nearby)

    def take(slot, row):
        picked[pl.ds(slot, 1), :] = spring[pl.ds(row, 1), :]
        for part in range(2):
            base[part, pl.ds(slot, 1), :] = nearby[part, pl.ds(row, 1), :]

    each_entry(chunks, rows, field.shape[1], take)
    relate(rows_line, stiff, picked, column, same, weight, factor, chunks, field.shape[1])


def scatter_inner_kernel(chunks, rows, entry, stale, field, nearby, base):
    def put(slot, row):
        for part in range(2):
            field[part, pl.ds(row, 1), :] = entry[part, pl.ds(slot, 1), :]

    each_slot(rows.shape[1], lambda j: rows[0, j], put)
    strips_all(chunks, field, nearby)

    def take(slot, row):
        for part in range(2):
            base[part, pl.ds(slot, 1), :] = nearby[part, pl.ds(row, 1), :]

    each_entry(chunks, rows, field.shape[1], take)


def settle_kernel(chunks, got_a, got_b, entry, raw, same, weight, factor, stiff, stale, nearby, base):
    count = stiff.shape[0]
    halos = halo_rows(got_a, got_b)
    add_halo(nearby, halos, chunks)
    unused = same.shape[1] - count - 2 * chunks
    edges = jnp.concatenate(
        [
            jnp.concatenate([above, below, jnp.zeros((unused, LANES), jnp.float32)], axis=0)
            for above, below in halos
        ],
        axis=1,
    )
    outside = summed(same[:, count:], edges)
    for part in range(2):
        value = entry[part]
        base[part] = value + weight[...] * (
            (raw[part] - value) + outside[:, part * LANES : (part + 1) * LANES]
        )


def new_entries(got_x, got_z, old, base, same, factor, stiff):
    matches = got_x.shape[1]
    count = 2 * matches
    term = jnp.concatenate(
        [
            jnp.concatenate(
                [
                    got[part] - stiff[at : at + matches, :] * old[part, at : at + matches, :]
                    for at, got in ((0, got_x), (matches, got_z))
                ],
                axis=0,
            )
            for part in range(2)
        ],
        axis=1,
    )
    total = summed(same[:, :count], term)
    return [base[part] + factor[...] * total[:, part * LANES : (part + 1) * LANES] for part in range(2)]


def step_kernel(got_x, got_z, old, base, same, factor, stiff, entry, send_x, send_z, edges):
    matches = got_x.shape[1]
    count = 2 * matches
    for part, value in enumerate(new_entries(got_x, got_z, old, base, same, factor, stiff)):
        entry[part] = value
        send_x[part] = value[:matches] * stiff[:matches, :]
        send_z[part] = value[matches:count] * stiff[matches:, :]
    edges[...] = entry[:, count:, :]


def last_kernel(rows, stale, got_x, got_z, old, base, same, factor, stiff, nearby, out, entry, sem):
    for part, value in enumerate(new_entries(got_x, got_z, old, base, same, factor, stiff)):
        entry[part] = value
    stores = load_parts(nearby, out, sem, LOADS)
    for part in range(2):

        def put(slot, row):
            nearby[part, pl.ds(row, 1), :] = entry[part, pl.ds(slot, 1), :]

        each_slot(rows.shape[1], lambda j: rows[0, j], put)
        for copy in stores[part * LOADS : (part + 1) * LOADS]:
            copy.start()
    for copy in stores:
        copy.wait()


def exchange(array, axis, pairs):
    return lax.ppermute(array, axis, pairs)


def pairs_from(first, size):
    out = []
    for i in range(first, size - 1, 2):
        out += [(i, i + 1), (i + 1, i)]
    return out


def on_device(displacement, spring, stiff_table, match_blocks, match_class):
    fields, _, height, breadth = displacement.shape
    chunks = breadth // LANES
    blocks = height * chunks
    matches = match_blocks.shape[2]
    count = 2 * matches
    total = count + 2 * chunks
    sections, tiles = lax.axis_size("sec"), lax.axis_size("tile")
    near, far = pairs_from(0, sections), pairs_from(1, sections)
    near_tile = pairs_from(0, tiles)
    relay = [(i - 1, i + 1) for i in range(1, tiles - 1, 2)] + [(i + 2, i) for i in range(1, tiles - 1, 2)]
    senders, takers = {a for a, _ in relay}, {b for _, b in relay}
    relay += [(b, a) for a, b in relay if b not in senders and a not in takers]

    def tiled(x):
        lead = x.shape[:-2]
        x = x.reshape(lead + (height // SUB, SUB, chunks, LANES))
        return jnp.swapaxes(x, -3, -2).reshape(lead + (blocks, LANES))

    def untiled(x):
        lead = x.shape[:-2]
        x = x.reshape(lead + (height // SUB, chunks, SUB, LANES))
        return jnp.swapaxes(x, -3, -2).reshape(lead + (height, breadth))

    def call(kernel, ins, outs, vmem=24 << 20, **more):
        return pl.pallas_call(
            kernel,
            in_specs=ins,
            out_specs=tuple(spec for spec, _ in outs),
            out_shape=tuple(shape for _, shape in outs),
            compiler_params=pltpu.CompilerParams(vmem_limit_bytes=vmem),
            **more,
        )

    halo = (VM, f32(fields, 2 * chunks, LANES))
    send = (VM, f32(fields, matches, LANES))
    entries = (VM, f32(fields, total, LANES))
    big = (VM, f32(fields, blocks, LANES))
    wide = (VM, f32(total, LANES))
    rows_shape = (VM, jax.ShapeDtypeStruct((1, count), jnp.int32))

    packed = jnp.concatenate([match_blocks, match_class[:, None]], axis=0)
    prev = exchange(packed, "sec", [(i, i + 1) for i in range(sections - 1)])
    staging = [
        pltpu.VMEM((1, matches), jnp.int32),
        pltpu.SMEM((1, matches), jnp.int32),
    ]
    field, own_entry = call(
        functools.partial(own_kernel, chunks),
        [VM, HBM],
        [big, send],
        scratch_shapes=staging + [pltpu.SemaphoreType.DMA, pltpu.SemaphoreType.DMA((2 * LOADS,))],
        vmem=OWN_VMEM << 20,
    )(packed, tiled(displacement[:, 0]))
    entry, stiff, rows, send_x, send_z, edges = call(
        functools.partial(first_kernel, chunks),
        [VM] * 5,
        [entries, (VM, f32(count, LANES)), rows_shape, send, send, halo],
        scratch_shapes=staging
        + [pltpu.VMEM((fields, matches, LANES), jnp.float32), pltpu.SemaphoreType.DMA],
    )(stiff_table[None], packed, prev, field, own_entry)

    for sweep in range(ITERS):
        got_x = exchange(send_x, "sec", near)
        got_z = exchange(send_z, "sec", far)
        got_a = exchange(edges, "tile", near_tile)
        got_b = exchange(got_a, "tile", relay)
        if sweep == 0:
            nearby, base, same, weight, factor = call(
                functools.partial(start_kernel, chunks),
                [SM, VM, VM, VM, VM],
                [big, entries, (VM, jax.ShapeDtypeStruct((total, count + LANES), jnp.bfloat16)), wide, wide],
                scratch_shapes=[pltpu.VMEM((total, LANES), jnp.float32)] * 2,
            )(rows, rows, stiff, tiled(spring[0]), field)
        else:
            field, nearby, base = call(
                functools.partial(scatter_inner_kernel, chunks),
                [SM] + [VM] * 2,
                [big, big, entries],
                input_output_aliases={2: 0},
            )(rows, entry, nearby)
        nearby, base = call(
            functools.partial(settle_kernel, chunks), [VM] * 9, [big, entries], input_output_aliases={8: 0}
        )(got_a, got_b, entry, base, same, weight, factor, stiff, nearby)
        if sweep < ITERS - 1:
            entry, send_x, send_z, edges = call(
                step_kernel, [VM] * 7, [entries, send, send, halo]
            )(got_x, got_z, entry, base, same, factor, stiff)
    _, out = call(
        last_kernel,
        [SM] + [VM] * 8,
        [big, (HBM, f32(fields, blocks, LANES))],
        scratch_shapes=[
            pltpu.VMEM((fields, total, LANES), jnp.float32),
            pltpu.SemaphoreType.DMA((2 * LOADS,)),
        ],
        input_output_aliases={1: 0},
    )(rows, nearby, got_x, got_z, entry, base, same, factor, stiff)
    return untiled(out)[:, None]


def solution(mesh):
    placed = (
        P(None, "sec", "tile", None),
        P("sec", "tile", None),
        P(),
        P(None, "sec", "tile"),
        P("sec", "tile"),
    )
    return jax.shard_map(
        on_device,
        mesh=mesh,
        in_specs=placed,
        out_specs=P(None, "sec", "tile", None),
        check_vma=False,
    )
```

profile of v0, /device:TPU:0, one launch (start us, length us, event | category | flops | bytes accessed | tf_op | source)
XLA Modules:
  0.0 53.0 jit_solution(13273797853618688904)
XLA Ops:
  0.0 0.0 copy-start.1
  0.0 0.7 %pad_add_fusion.packed = s32[3,1,256]{2,1,0:T(1,128)S(1)} fusion(s32[1,1,256]{2,1,0:T(1,128)} %bitcast.20, s32[2,1,256]{2,1,0:T(1,128)} %param.8), kind=kLoop, calls=%fused_computation | loop fusion | flops 768 | bytes 6144 | tf_op jit(solution)/shard_map/concatenate | solution.py:411
  0.7 4.9 %collective-permute-start = (s32[3,1,256]{2,1,0:T(1,128)S(1)}, s32[3,1,256]{2,1,0:T(1,128)S(1)}, u32[]{:S(2)}, u32[]{:S(2)}) collective-permute-start(s32[3,1,256]{2,1,0:T(1,128)S(1)} %pad_add_fusion.packed), channel_id=1, source_target_pairs={{0,4},{4,8},{8,12},{12,16},{16,20},{20,24},{24,28},{1,5},{5,9},{9,... | collective-permute-start | bytes 9224 | tf_op jit(solution)/shard_map/ppermute | solution.py:360
  5.6 0.0 copy-start
  5.6 2.6 %shard_map.55 = (f32[2,4096,128]{2,1,0:T(8,128)S(1)}, f32[2,256,128]{2,1,0:T(8,128)S(1)}) custom-call(s32[3,1,256]{2,1,0:T(1,128)S(1)} %pad_add_fusion.packed, f32[2,4096,128]{2,1,0:T(8,128)} %bitcast.19), custom_call_target="tpu_custom_call" | custom-call | tf_op jit(solution)/shard_map/pallas_call | solution.py:417
  8.2 0.0 collective-permute-done.prev
  8.2 0.0 copy-done.1
  8.3 1.1 %shard_map.56 = (f32[2,544,128]{2,1,0:T(8,128)S(1)}, f32[512,128]{1,0:T(8,128)S(1)}, s32[1,512]{1,0:T(1,128)S(1)}, f32[2,256,128]{2,1,0:T(8,128)S(1)}, f32[2,256...) custom-call(f32[1,8]{1,0:T(1,128)S(1)} %bitcast.18, s32[3,1,256]{2,1,0:T(1,128)S(1)} %pad_add_fusion.packed, ...), custom_call_target="tpu_custom_call" | custom-call | tf_op jit(solution)/shard_map/pallas_call | solution.py:424
  9.3 1.6 %collective-permute-start.1 = (f32[2,256,128]{2,1,0:T(8,128)S(1)}, f32[2,256,128]{2,1,0:T(8,128)S(1)}, u32[]{:S(2)}, u32[]{:S(2)}) collective-permute-start(f32[2,256,128]{2,1,0:T(8,128)S(1)} %get-tuple-element.40), channel_id=1, source_target_pairs={{0,4},{4,0},{8,12},{12,8},{16,20},{20,16},{24,28},{28,24},{1,5},{5... | collective-permute-start | bytes 786440 | tf_op jit(solution)/shard_map/ppermute | solution.py:360
  11.0 0.7 %collective-permute-start.2 = (f32[2,256,128]{2,1,0:T(8,128)S(1)}, f32[2,256,128]{2,1,0:T(8,128)S(1)}, u32[]{:S(2)}, u32[]{:S(2)}) collective-permute-start(f32[2,256,128]{2,1,0:T(8,128)S(1)} %get-tuple-element.41), channel_id=1, source_target_pairs={{4,8},{8,4},{12,16},{16,12},{20,24},{24,20},{5,9},{9,5},{13,17},{1... | collective-permute-start | bytes 786440 | tf_op jit(solution)/shard_map/ppermute | solution.py:360
  11.6 0.1 collective-permute-start.3
  11.7 1.2 %collective-permute-done.3.got_a = f32[2,32,128]{2,1,0:T(8,128)S(1)} collective-permute-done((f32[2,32,128]{2,1,0:T(8,128)S(1)}, f32[2,32,128]{2,1,0:T(8,128)S(1)}, u32[]{:S(2)}, u32[]{:S(2)}) %collective-permute-start.3) | collective-permute-done | bytes 32800 | tf_op jit(solution)/shard_map/ppermute | solution.py:360
  12.9 1.5 %collective-permute-start.4 = (f32[2,32,128]{2,1,0:T(8,128)S(1)}, f32[2,32,128]{2,1,0:T(8,128)S(1)}, u32[]{:S(2)}, u32[]{:S(2)}) collective-permute-start(f32[2,32,128]{2,1,0:T(8,128)S(1)} %collective-permute-done.3.got_a), channel_id=1, source_target_pairs={{0,2},{3,1},{2,0},{1,3},{4,6},{7,5},{6,4},{5,7},{8,10},{11,9},{10,... | collective-permute-start | bytes 98312 | tf_op jit(solution)/shard_map/ppermute | solution.py:360
  14.4 0.0 copy-done
  14.4 5.1 %shard_map.57 = (f32[2,4096,128]{2,1,0:T(8,128)S(1)}, f32[2,544,128]{2,1,0:T(8,128)S(1)}, bf16[544,640]{1,0:T(8,128)(2,1)S(1)}, f32[544,128]{1,0:T(8,128)S(1)}, f32[544,128]{1,0:T(8,128)S(1)}) custom-call(s32[1,512]{1,0:T(1,128)S(1)} %get-tuple-element.39.rows.rows_line, s32[1,512]{1,0:T(1,128)S(1)} %get-tuple-element.39.rows.rows_line, ...), custom_call_target="tpu_custom_call" | custom-call | tf_op jit(solution)/shard_map/pallas_call | solution.py:438
  19.5 0.0 collective-permute-done.4.got_b
  19.5 0.3 shard_map.58
  19.8 2.0 %collective-permute-done.1.got_x = f32[2,256,128]{2,1,0:T(8,128)S(1)} collective-permute-done((f32[2,256,128]{2,1,0:T(8,128)S(1)}, f32[2,256,128]{2,1,0:T(8,128)S(1)}, u32[]{:S(2)}, u32[]{:S(2)}) %collective-permute-start.1) | collective-permute-done | bytes 262176 | tf_op jit(solution)/shard_map/ppermute | solution.py:360
  21.9 0.0 collective-permute-done.2.got_z
  21.9 0.5 shard_map.59
  22.4 2.5 %collective-permute-start.5 = (f32[2,256,128]{2,1,0:T(8,128)S(1)}, f32[2,256,128]{2,1,0:T(8,128)S(1)}, u32[]{:S(2)}, u32[]{:S(2)}) collective-permute-start(f32[2,256,128]{2,1,0:T(8,128)S(1)} %get-tuple-element.51), channel_id=1, source_target_pairs={{0,4},{4,0},{8,12},{12,8},{16,20},{20,16},{24,28},{28,24},{1,5},{5... | collective-permute-start | bytes 786440 | tf_op jit(solution)/shard_map/ppermute | solution.py:360
  24.9 0.7 %collective-permute-start.6 = (f32[2,256,128]{2,1,0:T(8,128)S(1)}, f32[2,256,128]{2,1,0:T(8,128)S(1)}, u32[]{:S(2)}, u32[]{:S(2)}) collective-permute-start(f32[2,256,128]{2,1,0:T(8,128)S(1)} %get-tuple-element.52), channel_id=1, source_target_pairs={{4,8},{8,4},{12,16},{16,12},{20,24},{24,20},{5,9},{9,5},{13,17},{1... | collective-permute-start | bytes 786440 | tf_op jit(solution)/shard_map/ppermute | solution.py:360
  25.6 0.1 collective-permute-start.7
  25.7 1.2 %collective-permute-done.7.got_a = f32[2,32,128]{2,1,0:T(8,128)S(1)} collective-permute-done((f32[2,32,128]{2,1,0:T(8,128)S(1)}, f32[2,32,128]{2,1,0:T(8,128)S(1)}, u32[]{:S(2)}, u32[]{:S(2)}) %collective-permute-start.7) | collective-permute-done | bytes 32800 | tf_op jit(solution)/shard_map/ppermute | solution.py:360
  26.9 1.5 %collective-permute-start.8 = (f32[2,32,128]{2,1,0:T(8,128)S(1)}, f32[2,32,128]{2,1,0:T(8,128)S(1)}, u32[]{:S(2)}, u32[]{:S(2)}) collective-permute-start(f32[2,32,128]{2,1,0:T(8,128)S(1)} %collective-permute-done.7.got_a), channel_id=1, source_target_pairs={{0,2},{3,1},{2,0},{1,3},{4,6},{7,5},{6,4},{5,7},{8,10},{11,9},{10,... | collective-permute-start | bytes 98312 | tf_op jit(solution)/shard_map/ppermute | solution.py:360
  28.4 4.5 %shard_map.60 = (f32[2,4096,128]{2,1,0:T(8,128)S(1)}, f32[2,4096,128]{2,1,0:T(8,128)S(1)}, f32[2,544,128]{2,1,0:T(8,128)S(1)}) custom-call(s32[1,512]{1,0:T(1,128)S(1)} %get-tuple-element.39.rows.rows_line, f32[2,544,128]{2,1,0:T(8,128)S(1)} %get-tuple-element.53.entry.old, f32[2,4096,128]{2,1,0:T(8,128)S(1)} %get-tuple-element.55.stale), custom_call_target="tpu_custom_call", output_to_operand_aliasing={{0}: (2, {})} | custom-call | tf_op jit(solution)/shard_map/pallas_call | solution.py:445
  32.9 0.0 collective-permute-done.8.got_b
  32.9 0.4 shard_map.61
  33.2 2.7 %collective-permute-done.5.got_x = f32[2,256,128]{2,1,0:T(8,128)S(1)} collective-permute-done((f32[2,256,128]{2,1,0:T(8,128)S(1)}, f32[2,256,128]{2,1,0:T(8,128)S(1)}, u32[]{:S(2)}, u32[]{:S(2)}) %collective-permute-start.5) | collective-permute-done | bytes 262176 | tf_op jit(solution)/shard_map/ppermute | solution.py:360
  36.0 0.0 collective-permute-done.6.got_z
  36.0 0.5 shard_map.62
  36.5 2.6 %collective-permute-start.11 = (f32[2,256,128]{2,1,0:T(8,128)S(1)}, f32[2,256,128]{2,1,0:T(8,128)S(1)}, u32[]{:S(2)}, u32[]{:S(2)}) collective-permute-start(f32[2,256,128]{2,1,0:T(8,128)S(1)} %get-tuple-element.65), channel_id=1, source_target_pairs={{0,4},{4,0},{8,12},{12,8},{16,20},{20,16},{24,28},{28,24},{1,5},{5... | collective-permute-start | bytes 786440 | tf_op jit(solution)/shard_map/ppermute | solution.py:360
  39.0 0.7 %collective-permute-start.12 = (f32[2,256,128]{2,1,0:T(8,128)S(1)}, f32[2,256,128]{2,1,0:T(8,128)S(1)}, u32[]{:S(2)}, u32[]{:S(2)}) collective-permute-start(f32[2,256,128]{2,1,0:T(8,128)S(1)} %get-tuple-element.66), channel_id=1, source_target_pairs={{4,8},{8,4},{12,16},{16,12},{20,24},{24,20},{5,9},{9,5},{13,17},{1... | collective-permute-start | bytes 786440 | tf_op jit(solution)/shard_map/ppermute | solution.py:360
  39.7 0.1 collective-permute-start.9
  39.8 1.2 %collective-permute-done.9.got_a = f32[2,32,128]{2,1,0:T(8,128)S(1)} collective-permute-done((f32[2,32,128]{2,1,0:T(8,128)S(1)}, f32[2,32,128]{2,1,0:T(8,128)S(1)}, u32[]{:S(2)}, u32[]{:S(2)}) %collective-permute-start.9) | collective-permute-done | bytes 32800 | tf_op jit(solution)/shard_map/ppermute | solution.py:360
  41.0 0.5 collective-permute-start.10
  41.5 4.5 %shard_map.63 = (f32[2,4096,128]{2,1,0:T(8,128)S(1)}, f32[2,4096,128]{2,1,0:T(8,128)S(1)}, f32[2,544,128]{2,1,0:T(8,128)S(1)}) custom-call(s32[1,512]{1,0:T(1,128)S(1)} %get-tuple-element.39.rows.rows_line, f32[2,544,128]{2,1,0:T(8,128)S(1)} %get-tuple-element.60.entry.old, f32[2,4096,128]{2,1,0:T(8,128)S(1)} %get-tuple-element.61.stale), custom_call_target="tpu_custom_call", output_to_operand_aliasing={{0}: (2, {})} | custom-call | tf_op jit(solution)/shard_map/pallas_call | solution.py:445
  46.0 0.0 collective-permute-done.10.got_b
  46.0 0.3 shard_map.64
  46.3 3.0 %collective-permute-done.11.got_x = f32[2,256,128]{2,1,0:T(8,128)S(1)} collective-permute-done((f32[2,256,128]{2,1,0:T(8,128)S(1)}, f32[2,256,128]{2,1,0:T(8,128)S(1)}, u32[]{:S(2)}, u32[]{:S(2)}) %collective-permute-start.11) | collective-permute-done | bytes 262176 | tf_op jit(solution)/shard_map/ppermute | solution.py:360
  49.3 0.0 collective-permute-done.12.got_z
  49.3 3.7 %shard_map.65 = (f32[2,4096,128]{2,1,0:T(8,128)S(1)}, f32[2,4096,128]{2,1,0:T(8,128)}) custom-call(s32[1,512]{1,0:T(1,128)S(1)} %get-tuple-element.39.rows.rows_line, f32[2,4096,128]{2,1,0:T(8,128)S(1)} %get-tuple-element.64.stale, f32[2,256,128]{2,1,0:T(8,128)S(1)} %collective-permute-done.11.got_x, ...), custom_call_target="tpu_custom_call", output_to_operand_aliasing={{0}: (1, {})} | custom-call | tf_op jit(solution)/shard_map/pallas_call | solution.py:458
Async XLA Ops:
  0.0 8.2 %copy-start.1 = (f32[8]{0:T(128)S(1)}, f32[8]{0:T(128)}, u32[]{:S(2)}) copy-start(f32[8]{0:T(128)} %param.7) | copy-start | bytes 100
  0.7 7.5 %collective-permute-start = (s32[3,1,256]{2,1,0:T(1,128)S(1)}, s32[3,1,256]{2,1,0:T(1,128)S(1)}, u32[]{:S(2)}, u32[]{:S(2)}) collective-permute-start(s32[3,1,256]{2,1,0:T(1,128)S(1)} %pad_add_fusion.packed), channel_id=1, source_target_pairs={{0,4},{4,8},{8,12},{12,16},{16,20},{20,24},{24,28},{1,5},{5,9},{9,... | collective-permute-start | bytes 9224 | tf_op jit(solution)/shard_map/ppermute | solution.py:360
  5.6 8.8 %copy-start = (f32[1,256,2048]{2,1,0:T(8,128)S(1)}, f32[1,256,2048]{2,1,0:T(8,128)}, u32[]{:S(2)}) copy-start(f32[1,256,2048]{2,1,0:T(8,128)} %param.6) | copy-start | bytes 6291460
  9.3 12.5 %collective-permute-start.1 = (f32[2,256,128]{2,1,0:T(8,128)S(1)}, f32[2,256,128]{2,1,0:T(8,128)S(1)}, u32[]{:S(2)}, u32[]{:S(2)}) collective-permute-start(f32[2,256,128]{2,1,0:T(8,128)S(1)} %get-tuple-element.40), channel_id=1, source_target_pairs={{0,4},{4,0},{8,12},{12,8},{16,20},{20,16},{24,28},{28,24},{1,5},{5... | collective-permute-start | bytes 786440 | tf_op jit(solution)/shard_map/ppermute | solution.py:360
  11.0 10.9 %collective-permute-start.2 = (f32[2,256,128]{2,1,0:T(8,128)S(1)}, f32[2,256,128]{2,1,0:T(8,128)S(1)}, u32[]{:S(2)}, u32[]{:S(2)}) collective-permute-start(f32[2,256,128]{2,1,0:T(8,128)S(1)} %get-tuple-element.41), channel_id=1, source_target_pairs={{4,8},{8,4},{12,16},{16,12},{20,24},{24,20},{5,9},{9,5},{13,17},{1... | collective-permute-start | bytes 786440 | tf_op jit(solution)/shard_map/ppermute | solution.py:360
  11.6 1.3 %collective-permute-start.3 = (f32[2,32,128]{2,1,0:T(8,128)S(1)}, f32[2,32,128]{2,1,0:T(8,128)S(1)}, u32[]{:S(2)}, u32[]{:S(2)}) collective-permute-start(f32[2,32,128]{2,1,0:T(8,128)S(1)} %get-tuple-element.43), channel_id=1, source_target_pairs={{0,1},{1,0},{2,3},{3,2},{4,5},{5,4},{6,7},{7,6},{8,9},{9,8},{10,11... | collective-permute-start | bytes 98312 | tf_op jit(solution)/shard_map/ppermute | solution.py:360
  12.9 6.6 %collective-permute-start.4 = (f32[2,32,128]{2,1,0:T(8,128)S(1)}, f32[2,32,128]{2,1,0:T(8,128)S(1)}, u32[]{:S(2)}, u32[]{:S(2)}) collective-permute-start(f32[2,32,128]{2,1,0:T(8,128)S(1)} %collective-permute-done.3.got_a), channel_id=1, source_target_pairs={{0,2},{3,1},{2,0},{1,3},{4,6},{7,5},{6,4},{5,7},{8,10},{11,9},{10,... | collective-permute-start | bytes 98312 | tf_op jit(solution)/shard_map/ppermute | solution.py:360
  22.4 13.6 %collective-permute-start.5 = (f32[2,256,128]{2,1,0:T(8,128)S(1)}, f32[2,256,128]{2,1,0:T(8,128)S(1)}, u32[]{:S(2)}, u32[]{:S(2)}) collective-permute-start(f32[2,256,128]{2,1,0:T(8,128)S(1)} %get-tuple-element.51), channel_id=1, source_target_pairs={{0,4},{4,0},{8,12},{12,8},{16,20},{20,16},{24,28},{28,24},{1,5},{5... | collective-permute-start | bytes 786440 | tf_op jit(solution)/shard_map/ppermute | solution.py:360
  24.9 11.0 %collective-permute-start.6 = (f32[2,256,128]{2,1,0:T(8,128)S(1)}, f32[2,256,128]{2,1,0:T(8,128)S(1)}, u32[]{:S(2)}, u32[]{:S(2)}) collective-permute-start(f32[2,256,128]{2,1,0:T(8,128)S(1)} %get-tuple-element.52), channel_id=1, source_target_pairs={{4,8},{8,4},{12,16},{16,12},{20,24},{24,20},{5,9},{9,5},{13,17},{1... | collective-permute-start | bytes 786440 | tf_op jit(solution)/shard_map/ppermute | solution.py:360
  25.6 1.3 %collective-permute-start.7 = (f32[2,32,128]{2,1,0:T(8,128)S(1)}, f32[2,32,128]{2,1,0:T(8,128)S(1)}, u32[]{:S(2)}, u32[]{:S(2)}) collective-permute-start(f32[2,32,128]{2,1,0:T(8,128)S(1)} %get-tuple-element.54), channel_id=1, source_target_pairs={{0,1},{1,0},{2,3},{3,2},{4,5},{5,4},{6,7},{7,6},{8,9},{9,8},{10,11... | collective-permute-start | bytes 98312 | tf_op jit(solution)/shard_map/ppermute | solution.py:360
  26.9 6.0 %collective-permute-start.8 = (f32[2,32,128]{2,1,0:T(8,128)S(1)}, f32[2,32,128]{2,1,0:T(8,128)S(1)}, u32[]{:S(2)}, u32[]{:S(2)}) collective-permute-start(f32[2,32,128]{2,1,0:T(8,128)S(1)} %collective-permute-done.7.got_a), channel_id=1, source_target_pairs={{0,2},{3,1},{2,0},{1,3},{4,6},{7,5},{6,4},{5,7},{8,10},{11,9},{10,... | collective-permute-start | bytes 98312 | tf_op jit(solution)/shard_map/ppermute | solution.py:360
  36.5 12.8 %collective-permute-start.11 = (f32[2,256,128]{2,1,0:T(8,128)S(1)}, f32[2,256,128]{2,1,0:T(8,128)S(1)}, u32[]{:S(2)}, u32[]{:S(2)}) collective-permute-start(f32[2,256,128]{2,1,0:T(8,128)S(1)} %get-tuple-element.65), channel_id=1, source_target_pairs={{0,4},{4,0},{8,12},{12,8},{16,20},{20,16},{24,28},{28,24},{1,5},{5... | collective-permute-start | bytes 786440 | tf_op jit(solution)/shard_map/ppermute | solution.py:360
  39.0 10.3 %collective-permute-start.12 = (f32[2,256,128]{2,1,0:T(8,128)S(1)}, f32[2,256,128]{2,1,0:T(8,128)S(1)}, u32[]{:S(2)}, u32[]{:S(2)}) collective-permute-start(f32[2,256,128]{2,1,0:T(8,128)S(1)} %get-tuple-element.66), channel_id=1, source_target_pairs={{4,8},{8,4},{12,16},{16,12},{20,24},{24,20},{5,9},{9,5},{13,17},{1... | collective-permute-start | bytes 786440 | tf_op jit(solution)/shard_map/ppermute | solution.py:360
  39.7 1.3 %collective-permute-start.9 = (f32[2,32,128]{2,1,0:T(8,128)S(1)}, f32[2,32,128]{2,1,0:T(8,128)S(1)}, u32[]{:S(2)}, u32[]{:S(2)}) collective-permute-start(f32[2,32,128]{2,1,0:T(8,128)S(1)} %get-tuple-element.59), channel_id=1, source_target_pairs={{0,1},{1,0},{2,3},{3,2},{4,5},{5,4},{6,7},{7,6},{8,9},{9,8},{10,11... | collective-permute-start | bytes 98312 | tf_op jit(solution)/shard_map/ppermute | solution.py:360
  41.0 5.0 %collective-permute-start.10 = (f32[2,32,128]{2,1,0:T(8,128)S(1)}, f32[2,32,128]{2,1,0:T(8,128)S(1)}, u32[]{:S(2)}, u32[]{:S(2)}) collective-permute-start(f32[2,32,128]{2,1,0:T(8,128)S(1)} %collective-permute-done.9.got_a), channel_id=1, source_target_pairs={{0,2},{3,1},{2,0},{1,3},{4,6},{7,5},{6,4},{5,7},{8,10},{11,9},{10,... | collective-permute-start | bytes 98312 | tf_op jit(solution)/shard_map/ppermute | solution.py:360
where the time goes:
time: 53.2 us; the launch traced here: 53 us
  Pallas kernels  23.4 us (44%)
  starting transfers between devices  17.4 us (33%)
  waiting for transfers between devices  11.3 us (21%)
  other arithmetic  0.71 us (1%)
    ppermute x13, starting transfers between devices, exchange(): return lax.ppermute(array, axis, pairs)  17.4 us
    ppermute x13, waiting for transfers between devices, exchange(): return lax.ppermute(array, axis, pairs)  11.3 us
    pallas_call x2, Pallas kernels, on_device(): call(functools.partial(scatter_inner_kernel, chunks), [SM] + [VM] * 2, [b...  8.96 us
    pallas_call x1, Pallas kernels, on_device(): call(functools.partial(start_kernel, chunks), [SM, VM, VM, VM, VM], [big,...  5.07 us
    pallas_call x1, Pallas kernels, on_device(): call(last_kernel, [SM] + [VM] * 8, [big, (HBM, f32(fields, blocks, LANES)...  3.68 us
    pallas_call x1, Pallas kernels, on_device(): call(functools.partial(own_kernel, chunks), [VM, HBM], [big, send], scrat...  2.64 us
    pallas_call x1, Pallas kernels, on_device(): call(functools.partial(first_kernel, chunks), [VM] * 5, [entries, (VM, f3...  1.07 us
  transfers between devices with their start and end apart: 13, of which 6 were waited for; matrix products, arithmetic and copies ran while one was open for 0% of the time, Pallas kernels for 33%

commit v1 on v0

--- a/solution.py
+++ b/solution.py
@@ -8,8 +8,8 @@
 from jax.sharding import PartitionSpec as P
 
 ITERS = 3
-LOADS = 4
-GROUP = 6
+LOADS = 1
+GROUP = 15
 OWN_VMEM = 47
 LANES = 128
 SUB = 8
@@ -303,45 +303,39 @@
         axis=1,
     )
     outside = summed(same[:, count:], edges)
-    for part in range(2):
+    own = jnp.concatenate([entry[part, :count, :] * stiff[...] for part in range(2)], axis=1)
+    total = summed(same[:, :count], own)
+    for part in range(2):
+        cut = slice(part * LANES, (part + 1) * LANES)
         value = entry[part]
-        base[part] = value + weight[...] * (
-            (raw[part] - value) + outside[:, part * LANES : (part + 1) * LANES]
+        base[part] = (
+            value
+            + weight[...] * ((raw[part] - value) + outside[:, cut])
+            - factor[...] * total[:, cut]
         )
 
 
-def new_entries(got_x, got_z, old, base, same, factor, stiff):
+def new_entries(got_x, got_z, base, same, factor):
+    count = 2 * got_x.shape[1]
+    got = jnp.concatenate(
+        [jnp.concatenate([got_x[part], got_z[part]], axis=0) for part in range(2)], axis=1
+    )
+    total = summed(same[:, :count], got)
+    return [base[part] + factor[...] * total[:, part * LANES : (part + 1) * LANES] for part in range(2)]
+
+
+def step_kernel(got_x, got_z, base, same, factor, stiff, entry, send_x, send_z, edges):
     matches = got_x.shape[1]
     count = 2 * matches
-    term = jnp.concatenate(
-        [
-            jnp.concatenate(
-                [
-                    got[part] - stiff[at : at + matches, :] * old[part, at : at + matches, :]
-                    for at, got in ((0, got_x), (matches, got_z))
-                ],
-                axis=0,
-            )
-            for part in range(2)
-        ],
-        axis=1,
-    )
-    total = summed(same[:, :count], term)
-    return [base[part] + factor[...] * total[:, part * LANES : (part + 1) * LANES] for part in range(2)]
-
-
-def step_kernel(got_x, got_z, old, base, same, factor, stiff, entry, send_x, send_z, edges):
-    matches = got_x.shape[1]
-    count = 2 * matches
-    for part, value in enumerate(new_entries(got_x, got_z, old, base, same, factor, stiff)):
+    for part, value in enumerate(new_entries(got_x, got_z, base, same, factor)):
         entry[part] = value
         send_x[part] = value[:matches] * stiff[:matches, :]
         send_z[part] = value[matches:count] * stiff[matches:, :]
     edges[...] = entry[:, count:, :]
 
 
-def last_kernel(rows, stale, got_x, got_z, old, base, same, factor, stiff, nearby, out, entry, sem):
-    for part, value in enumerate(new_entries(got_x, got_z, old, base, same, factor, stiff)):
+def last_kernel(rows, stale, got_x, got_z, base, same, factor, nearby, out, entry, sem):
+    for part, value in enumerate(new_entries(got_x, got_z, base, same, factor)):
         entry[part] = value
     stores = load_parts(nearby, out, sem, LOADS)
     for part in range(2):
@@ -453,18 +447,18 @@
         )(got_a, got_b, entry, base, same, weight, factor, stiff, nearby)
         if sweep < ITERS - 1:
             entry, send_x, send_z, edges = call(
-                step_kernel, [VM] * 7, [entries, send, send, halo]
-            )(got_x, got_z, entry, base, same, factor, stiff)
+                step_kernel, [VM] * 6, [entries, send, send, halo]
+            )(got_x, got_z, base, same, factor, stiff)
     _, out = call(
         last_kernel,
-        [SM] + [VM] * 8,
+        [SM] + [VM] * 6,
         [big, (HBM, f32(fields, blocks, LANES))],
         scratch_shapes=[
             pltpu.VMEM((fields, total, LANES), jnp.float32),
             pltpu.SemaphoreType.DMA((2 * LOADS,)),
         ],
         input_output_aliases={1: 0},
-    )(rows, nearby, got_x, got_z, entry, base, same, factor, stiff)
+    )(rows, nearby, got_x, got_z, base, same, factor)
     return untiled(out)[:, None]
 
 

time: 53.2 us -> 53.3 us (level)
    pallas_call x3, Pallas kernels: 1.01 us -> 2.09 us  [on_device(): call(functools.partial(settle_kernel, chunks), [VM] * 9, [big, entries],...]
  transfers between devices with their start and end apart: 13 -> 13, of which waited for: 6 -> 6; matrix products, arithmetic and copies ran while one was open for 0% -> 0% of each run, Pallas kernels for 33% -> 34%
where the time goes in v1:
time: 53.3 us; the launch traced here: 53 us
  Pallas kernels  23.8 us (45%)
  starting transfers between devices  17.3 us (32%)
  waiting for transfers between devices  11 us (21%)
  other arithmetic  0.71 us (1%)
    ppermute x13, starting transfers between devices, exchange(): return lax.ppermute(array, axis, pairs)  17.3 us
    ppermute x13, waiting for transfers between devices, exchange(): return lax.ppermute(array, axis, pairs)  11 us
    pallas_call x2, Pallas kernels, on_device(): call(functools.partial(scatter_inner_kernel, chunks), [SM] + [VM] * 2, [b...  8.53 us
    pallas_call x1, Pallas kernels, on_device(): call(functools.partial(start_kernel, chunks), [SM, VM, VM, VM, VM], [big,...  4.86 us
    pallas_call x1, Pallas kernels, on_device(): call(last_kernel, [SM] + [VM] * 6, [big, (HBM, f32(fields, blocks, LANES)...  3.6 us
    pallas_call x1, Pallas kernels, on_device(): call(functools.partial(own_kernel, chunks), [VM, HBM], [big, send], scrat...  2.66 us
    pallas_call x3, Pallas kernels, on_device(): call(functools.partial(settle_kernel, chunks), [VM] * 9, [big, entries],...  2.09 us
    pallas_call x1, Pallas kernels, on_device(): call(functools.partial(first_kernel, chunks), [VM] * 5, [entries, (VM, f3...  1.07 us
  transfers between devices with their start and end apart: 13, of which 6 were waited for; matrix products, arithmetic and copies ran while one was open for 0% of the time, Pallas kernels for 34%

profile of v1, /device:TPU:0, one launch (start us, length us, event | category | flops | bytes accessed | tf_op | source)
XLA Modules:
  0.0 53.0 jit_solution(16396039018311019394)
XLA Ops:
  0.0 0.0 copy-start.1
  0.0 0.7 %pad_add_fusion.packed = s32[3,1,256]{2,1,0:T(1,128)S(1)} fusion(s32[1,1,256]{2,1,0:T(1,128)} %bitcast.20, s32[2,1,256]{2,1,0:T(1,128)} %param.8), kind=kLoop, calls=%fused_computation | loop fusion | flops 768 | bytes 6144 | tf_op jit(solution)/shard_map/concatenate | solution.py:405
  0.7 4.9 %collective-permute-start = (s32[3,1,256]{2,1,0:T(1,128)S(1)}, s32[3,1,256]{2,1,0:T(1,128)S(1)}, u32[]{:S(2)}, u32[]{:S(2)}) collective-permute-start(s32[3,1,256]{2,1,0:T(1,128)S(1)} %pad_add_fusion.packed), channel_id=1, source_target_pairs={{0,4},{4,8},{8,12},{12,16},{16,20},{20,24},{24,28},{1,5},{5,9},{9,... | collective-permute-start | bytes 9224 | tf_op jit(solution)/shard_map/ppermute | solution.py:354
  5.6 0.0 copy-start
  5.6 2.7 %shard_map.55 = (f32[2,4096,128]{2,1,0:T(8,128)S(1)}, f32[2,256,128]{2,1,0:T(8,128)S(1)}) custom-call(s32[3,1,256]{2,1,0:T(1,128)S(1)} %pad_add_fusion.packed, f32[2,4096,128]{2,1,0:T(8,128)} %bitcast.19), custom_call_target="tpu_custom_call" | custom-call | tf_op jit(solution)/shard_map/pallas_call | solution.py:411
  8.3 0.0 collective-permute-done.prev
  8.3 0.0 copy-done.1
  8.3 1.1 %shard_map.56 = (f32[2,544,128]{2,1,0:T(8,128)S(1)}, f32[512,128]{1,0:T(8,128)S(1)}, s32[1,512]{1,0:T(1,128)S(1)}, f32[2,256,128]{2,1,0:T(8,128)S(1)}, f32[2,256...) custom-call(f32[1,8]{1,0:T(1,128)S(1)} %bitcast.18, s32[3,1,256]{2,1,0:T(1,128)S(1)} %pad_add_fusion.packed, ...), custom_call_target="tpu_custom_call" | custom-call | tf_op jit(solution)/shard_map/pallas_call | solution.py:418
  9.4 1.6 %collective-permute-start.1 = (f32[2,256,128]{2,1,0:T(8,128)S(1)}, f32[2,256,128]{2,1,0:T(8,128)S(1)}, u32[]{:S(2)}, u32[]{:S(2)}) collective-permute-start(f32[2,256,128]{2,1,0:T(8,128)S(1)} %get-tuple-element.40), channel_id=1, source_target_pairs={{0,4},{4,0},{8,12},{12,8},{16,20},{20,16},{24,28},{28,24},{1,5},{5... | collective-permute-start | bytes 786440 | tf_op jit(solution)/shard_map/ppermute | solution.py:354
  11.0 0.7 %collective-permute-start.2 = (f32[2,256,128]{2,1,0:T(8,128)S(1)}, f32[2,256,128]{2,1,0:T(8,128)S(1)}, u32[]{:S(2)}, u32[]{:S(2)}) collective-permute-start(f32[2,256,128]{2,1,0:T(8,128)S(1)} %get-tuple-element.41), channel_id=1, source_target_pairs={{4,8},{8,4},{12,16},{16,12},{20,24},{24,20},{5,9},{9,5},{13,17},{1... | collective-permute-start | bytes 786440 | tf_op jit(solution)/shard_map/ppermute | solution.py:354
  11.7 0.1 collective-permute-start.3
  11.7 1.2 %collective-permute-done.3.got_a = f32[2,32,128]{2,1,0:T(8,128)S(1)} collective-permute-done((f32[2,32,128]{2,1,0:T(8,128)S(1)}, f32[2,32,128]{2,1,0:T(8,128)S(1)}, u32[]{:S(2)}, u32[]{:S(2)}) %collective-permute-start.3) | collective-permute-done | bytes 32800 | tf_op jit(solution)/shard_map/ppermute | solution.py:354
  12.9 1.5 %collective-permute-start.4 = (f32[2,32,128]{2,1,0:T(8,128)S(1)}, f32[2,32,128]{2,1,0:T(8,128)S(1)}, u32[]{:S(2)}, u32[]{:S(2)}) collective-permute-start(f32[2,32,128]{2,1,0:T(8,128)S(1)} %collective-permute-done.3.got_a), channel_id=1, source_target_pairs={{0,2},{3,1},{2,0},{1,3},{4,6},{7,5},{6,4},{5,7},{8,10},{11,9},{10,... | collective-permute-start | bytes 98312 | tf_op jit(solution)/shard_map/ppermute | solution.py:354
  14.4 0.0 copy-done
  14.4 4.9 %shard_map.57 = (f32[2,4096,128]{2,1,0:T(8,128)S(1)}, f32[2,544,128]{2,1,0:T(8,128)S(1)}, bf16[544,640]{1,0:T(8,128)(2,1)S(1)}, f32[544,128]{1,0:T(8,128)S(1)}, f32[544,128]{1,0:T(8,128)S(1)}) custom-call(s32[1,512]{1,0:T(1,128)S(1)} %get-tuple-element.39.rows.rows_line, s32[1,512]{1,0:T(1,128)S(1)} %get-tuple-element.39.rows.rows_line, ...), custom_call_target="tpu_custom_call" | custom-call | tf_op jit(solution)/shard_map/pallas_call | solution.py:432
  19.3 0.0 collective-permute-done.4.got_b
  19.3 0.7 %shard_map.58 = (f32[2,4096,128]{2,1,0:T(8,128)S(1)}, f32[2,544,128]{2,1,0:T(8,128)S(1)}) custom-call(f32[2,32,128]{2,1,0:T(8,128)S(1)} %collective-permute-done.3.got_a, f32[2,32,128]{2,1,0:T(8,128)S(1)} %collective-permute-done.4.got_b, f32[2,544,128]{2,1,0:T(8,128)S(1)} %get-tuple-element.43.entry, ...), custom_call_target="tpu_custom_call", output_to_operand_aliasing={{0}: (8, {})} | custom-call | tf_op jit(solution)/shard_map/pallas_call | solution.py:445
  20.0 1.9 %collective-permute-done.1.got_x = f32[2,256,128]{2,1,0:T(8,128)S(1)} collective-permute-done((f32[2,256,128]{2,1,0:T(8,128)S(1)}, f32[2,256,128]{2,1,0:T(8,128)S(1)}, u32[]{:S(2)}, u32[]{:S(2)}) %collective-permute-start.1) | collective-permute-done | bytes 262176 | tf_op jit(solution)/shard_map/ppermute | solution.py:354
  21.9 0.0 collective-permute-done.2.got_z
  21.9 0.5 shard_map.59
  22.4 2.5 %collective-permute-start.5 = (f32[2,256,128]{2,1,0:T(8,128)S(1)}, f32[2,256,128]{2,1,0:T(8,128)S(1)}, u32[]{:S(2)}, u32[]{:S(2)}) collective-permute-start(f32[2,256,128]{2,1,0:T(8,128)S(1)} %get-tuple-element.51), channel_id=1, source_target_pairs={{0,4},{4,0},{8,12},{12,8},{16,20},{20,16},{24,28},{28,24},{1,5},{5... | collective-permute-start | bytes 786440 | tf_op jit(solution)/shard_map/ppermute | solution.py:354
  24.9 0.7 %collective-permute-start.6 = (f32[2,256,128]{2,1,0:T(8,128)S(1)}, f32[2,256,128]{2,1,0:T(8,128)S(1)}, u32[]{:S(2)}, u32[]{:S(2)}) collective-permute-start(f32[2,256,128]{2,1,0:T(8,128)S(1)} %get-tuple-element.52), channel_id=1, source_target_pairs={{4,8},{8,4},{12,16},{16,12},{20,24},{24,20},{5,9},{9,5},{13,17},{1... | collective-permute-start | bytes 786440 | tf_op jit(solution)/shard_map/ppermute | solution.py:354
  25.6 0.1 collective-permute-start.7
  25.7 1.2 %collective-permute-done.7.got_a = f32[2,32,128]{2,1,0:T(8,128)S(1)} collective-permute-done((f32[2,32,128]{2,1,0:T(8,128)S(1)}, f32[2,32,128]{2,1,0:T(8,128)S(1)}, u32[]{:S(2)}, u32[]{:S(2)}) %collective-permute-start.7) | collective-permute-done | bytes 32800 | tf_op jit(solution)/shard_map/ppermute | solution.py:354
  26.9 1.5 %collective-permute-start.8 = (f32[2,32,128]{2,1,0:T(8,128)S(1)}, f32[2,32,128]{2,1,0:T(8,128)S(1)}, u32[]{:S(2)}, u32[]{:S(2)}) collective-permute-start(f32[2,32,128]{2,1,0:T(8,128)S(1)} %collective-permute-done.7.got_a), channel_id=1, source_target_pairs={{0,2},{3,1},{2,0},{1,3},{4,6},{7,5},{6,4},{5,7},{8,10},{11,9},{10,... | collective-permute-start | bytes 98312 | tf_op jit(solution)/shard_map/ppermute | solution.py:354
  28.4 4.3 %shard_map.60 = (f32[2,4096,128]{2,1,0:T(8,128)S(1)}, f32[2,4096,128]{2,1,0:T(8,128)S(1)}, f32[2,544,128]{2,1,0:T(8,128)S(1)}) custom-call(s32[1,512]{1,0:T(1,128)S(1)} %get-tuple-element.39.rows.rows_line, f32[2,544,128]{2,1,0:T(8,128)S(1)} %get-tuple-element.54.entry, f32[2,4096,128]{2,1,0:T(8,128)S(1)} %get-tuple-element.55.stale), custom_call_target="tpu_custom_call", output_to_operand_aliasing={{0}: (2, {})} | custom-call | tf_op jit(solution)/shard_map/pallas_call | solution.py:439
  32.7 0.0 collective-permute-done.8.got_b
  32.7 0.7 %shard_map.61 = (f32[2,4096,128]{2,1,0:T(8,128)S(1)}, f32[2,544,128]{2,1,0:T(8,128)S(1)}) custom-call(f32[2,32,128]{2,1,0:T(8,128)S(1)} %collective-permute-done.7.got_a, f32[2,32,128]{2,1,0:T(8,128)S(1)} %collective-permute-done.8.got_b, f32[2,544,128]{2,1,0:T(8,128)S(1)} %get-tuple-element.54.entry, ...), custom_call_target="tpu_custom_call", output_to_operand_aliasing={{0}: (8, {})} | custom-call | tf_op jit(solution)/shard_map/pallas_call | solution.py:445
  33.4 2.7 %collective-permute-done.5.got_x = f32[2,256,128]{2,1,0:T(8,128)S(1)} collective-permute-done((f32[2,256,128]{2,1,0:T(8,128)S(1)}, f32[2,256,128]{2,1,0:T(8,128)S(1)}, u32[]{:S(2)}, u32[]{:S(2)}) %collective-permute-start.5) | collective-permute-done | bytes 262176 | tf_op jit(solution)/shard_map/ppermute | solution.py:354
  36.1 0.0 collective-permute-done.6.got_z
  36.1 0.5 shard_map.62
  36.6 2.5 %collective-permute-start.11 = (f32[2,256,128]{2,1,0:T(8,128)S(1)}, f32[2,256,128]{2,1,0:T(8,128)S(1)}, u32[]{:S(2)}, u32[]{:S(2)}) collective-permute-start(f32[2,256,128]{2,1,0:T(8,128)S(1)} %get-tuple-element.65), channel_id=1, source_target_pairs={{0,4},{4,0},{8,12},{12,8},{16,20},{20,16},{24,28},{28,24},{1,5},{5... | collective-permute-start | bytes 786440 | tf_op jit(solution)/shard_map/ppermute | solution.py:354
  39.1 0.7 %collective-permute-start.12 = (f32[2,256,128]{2,1,0:T(8,128)S(1)}, f32[2,256,128]{2,1,0:T(8,128)S(1)}, u32[]{:S(2)}, u32[]{:S(2)}) collective-permute-start(f32[2,256,128]{2,1,0:T(8,128)S(1)} %get-tuple-element.66), channel_id=1, source_target_pairs={{4,8},{8,4},{12,16},{16,12},{20,24},{24,20},{5,9},{9,5},{13,17},{1... | collective-permute-start | bytes 786440 | tf_op jit(solution)/shard_map/ppermute | solution.py:354
  39.8 0.1 collective-permute-start.9
  39.9 1.2 %collective-permute-done.9.got_a = f32[2,32,128]{2,1,0:T(8,128)S(1)} collective-permute-done((f32[2,32,128]{2,1,0:T(8,128)S(1)}, f32[2,32,128]{2,1,0:T(8,128)S(1)}, u32[]{:S(2)}, u32[]{:S(2)}) %collective-permute-start.9) | collective-permute-done | bytes 32800 | tf_op jit(solution)/shard_map/ppermute | solution.py:354
  41.1 0.5 collective-permute-start.10
  41.6 4.3 %shard_map.63 = (f32[2,4096,128]{2,1,0:T(8,128)S(1)}, f32[2,4096,128]{2,1,0:T(8,128)S(1)}, f32[2,544,128]{2,1,0:T(8,128)S(1)}) custom-call(s32[1,512]{1,0:T(1,128)S(1)} %get-tuple-element.39.rows.rows_line, f32[2,544,128]{2,1,0:T(8,128)S(1)} %get-tuple-element.60.entry, f32[2,4096,128]{2,1,0:T(8,128)S(1)} %get-tuple-element.61.stale), custom_call_target="tpu_custom_call", output_to_operand_aliasing={{0}: (2, {})} | custom-call | tf_op jit(solution)/shard_map/pallas_call | solution.py:439
  45.8 0.0 collective-permute-done.10.got_b
  45.9 0.7 %shard_map.64 = (f32[2,4096,128]{2,1,0:T(8,128)S(1)}, f32[2,544,128]{2,1,0:T(8,128)S(1)}) custom-call(f32[2,32,128]{2,1,0:T(8,128)S(1)} %collective-permute-done.9.got_a, f32[2,32,128]{2,1,0:T(8,128)S(1)} %collective-permute-done.10.got_b, f32[2,544,128]{2,1,0:T(8,128)S(1)} %get-tuple-element.60.entry, ...), custom_call_target="tpu_custom_call", output_to_operand_aliasing={{0}: (8, {})} | custom-call | tf_op jit(solution)/shard_map/pallas_call | solution.py:445
  46.6 2.9 %collective-permute-done.11.got_x = f32[2,256,128]{2,1,0:T(8,128)S(1)} collective-permute-done((f32[2,256,128]{2,1,0:T(8,128)S(1)}, f32[2,256,128]{2,1,0:T(8,128)S(1)}, u32[]{:S(2)}, u32[]{:S(2)}) %collective-permute-start.11) | collective-permute-done | bytes 262176 | tf_op jit(solution)/shard_map/ppermute | solution.py:354
  49.4 0.0 collective-permute-done.12.got_z
  49.4 3.6 %shard_map.65 = (f32[2,4096,128]{2,1,0:T(8,128)S(1)}, f32[2,4096,128]{2,1,0:T(8,128)}) custom-call(s32[1,512]{1,0:T(1,128)S(1)} %get-tuple-element.39.rows.rows_line, f32[2,4096,128]{2,1,0:T(8,128)S(1)} %get-tuple-element.64.stale, f32[2,256,128]{2,1,0:T(8,128)S(1)} %collective-permute-done.11.got_x, ...), custom_call_target="tpu_custom_call", output_to_operand_aliasing={{0}: (1, {})} | custom-call | tf_op jit(solution)/shard_map/pallas_call | solution.py:452
Async XLA Ops:
  0.0 8.3 %copy-start.1 = (f32[8]{0:T(128)S(1)}, f32[8]{0:T(128)}, u32[]{:S(2)}) copy-start(f32[8]{0:T(128)} %param.7) | copy-start | bytes 100
  0.7 7.5 %collective-permute-start = (s32[3,1,256]{2,1,0:T(1,128)S(1)}, s32[3,1,256]{2,1,0:T(1,128)S(1)}, u32[]{:S(2)}, u32[]{:S(2)}) collective-permute-start(s32[3,1,256]{2,1,0:T(1,128)S(1)} %pad_add_fusion.packed), channel_id=1, source_target_pairs={{0,4},{4,8},{8,12},{12,16},{16,20},{20,24},{24,28},{1,5},{5,9},{9,... | collective-permute-start | bytes 9224 | tf_op jit(solution)/shard_map/ppermute | solution.py:354
  5.6 8.9 %copy-start = (f32[1,256,2048]{2,1,0:T(8,128)S(1)}, f32[1,256,2048]{2,1,0:T(8,128)}, u32[]{:S(2)}) copy-start(f32[1,256,2048]{2,1,0:T(8,128)} %param.6) | copy-start | bytes 6291460
  9.4 12.5 %collective-permute-start.1 = (f32[2,256,128]{2,1,0:T(8,128)S(1)}, f32[2,256,128]{2,1,0:T(8,128)S(1)}, u32[]{:S(2)}, u32[]{:S(2)}) collective-permute-start(f32[2,256,128]{2,1,0:T(8,128)S(1)} %get-tuple-element.40), channel_id=1, source_target_pairs={{0,4},{4,0},{8,12},{12,8},{16,20},{20,16},{24,28},{28,24},{1,5},{5... | collective-permute-start | bytes 786440 | tf_op jit(solution)/shard_map/ppermute | solution.py:354
  11.0 10.9 %collective-permute-start.2 = (f32[2,256,128]{2,1,0:T(8,128)S(1)}, f32[2,256,128]{2,1,0:T(8,128)S(1)}, u32[]{:S(2)}, u32[]{:S(2)}) collective-permute-start(f32[2,256,128]{2,1,0:T(8,128)S(1)} %get-tuple-element.41), channel_id=1, source_target_pairs={{4,8},{8,4},{12,16},{16,12},{20,24},{24,20},{5,9},{9,5},{13,17},{1... | collective-permute-start | bytes 786440 | tf_op jit(solution)/shard_map/ppermute | solution.py:354
  11.7 1.3 %collective-permute-start.3 = (f32[2,32,128]{2,1,0:T(8,128)S(1)}, f32[2,32,128]{2,1,0:T(8,128)S(1)}, u32[]{:S(2)}, u32[]{:S(2)}) collective-permute-start(f32[2,32,128]{2,1,0:T(8,128)S(1)} %get-tuple-element.42), channel_id=1, source_target_pairs={{0,1},{1,0},{2,3},{3,2},{4,5},{5,4},{6,7},{7,6},{8,9},{9,8},{10,11... | collective-permute-start | bytes 98312 | tf_op jit(solution)/shard_map/ppermute | solution.py:354
  12.9 6.4 %collective-permute-start.4 = (f32[2,32,128]{2,1,0:T(8,128)S(1)}, f32[2,32,128]{2,1,0:T(8,128)S(1)}, u32[]{:S(2)}, u32[]{:S(2)}) collective-permute-start(f32[2,32,128]{2,1,0:T(8,128)S(1)} %collective-permute-done.3.got_a), channel_id=1, source_target_pairs={{0,2},{3,1},{2,0},{1,3},{4,6},{7,5},{6,4},{5,7},{8,10},{11,9},{10,... | collective-permute-start | bytes 98312 | tf_op jit(solution)/shard_map/ppermute | solution.py:354
  22.4 13.7 %collective-permute-start.5 = (f32[2,256,128]{2,1,0:T(8,128)S(1)}, f32[2,256,128]{2,1,0:T(8,128)S(1)}, u32[]{:S(2)}, u32[]{:S(2)}) collective-permute-start(f32[2,256,128]{2,1,0:T(8,128)S(1)} %get-tuple-element.51), channel_id=1, source_target_pairs={{0,4},{4,0},{8,12},{12,8},{16,20},{20,16},{24,28},{28,24},{1,5},{5... | collective-permute-start | bytes 786440 | tf_op jit(solution)/shard_map/ppermute | solution.py:354
  24.9 11.2 %collective-permute-start.6 = (f32[2,256,128]{2,1,0:T(8,128)S(1)}, f32[2,256,128]{2,1,0:T(8,128)S(1)}, u32[]{:S(2)}, u32[]{:S(2)}) collective-permute-start(f32[2,256,128]{2,1,0:T(8,128)S(1)} %get-tuple-element.52), channel_id=1, source_target_pairs={{4,8},{8,4},{12,16},{16,12},{20,24},{24,20},{5,9},{9,5},{13,17},{1... | collective-permute-start | bytes 786440 | tf_op jit(solution)/shard_map/ppermute | solution.py:354
  25.6 1.3 %collective-permute-start.7 = (f32[2,32,128]{2,1,0:T(8,128)S(1)}, f32[2,32,128]{2,1,0:T(8,128)S(1)}, u32[]{:S(2)}, u32[]{:S(2)}) collective-permute-start(f32[2,32,128]{2,1,0:T(8,128)S(1)} %get-tuple-element.53), channel_id=1, source_target_pairs={{0,1},{1,0},{2,3},{3,2},{4,5},{5,4},{6,7},{7,6},{8,9},{9,8},{10,11... | collective-permute-start | bytes 98312 | tf_op jit(solution)/shard_map/ppermute | solution.py:354
  26.9 5.8 %collective-permute-start.8 = (f32[2,32,128]{2,1,0:T(8,128)S(1)}, f32[2,32,128]{2,1,0:T(8,128)S(1)}, u32[]{:S(2)}, u32[]{:S(2)}) collective-permute-start(f32[2,32,128]{2,1,0:T(8,128)S(1)} %collective-permute-done.7.got_a), channel_id=1, source_target_pairs={{0,2},{3,1},{2,0},{1,3},{4,6},{7,5},{6,4},{5,7},{8,10},{11,9},{10,... | collective-permute-start | bytes 98312 | tf_op jit(solution)/shard_map/ppermute | solution.py:354
  36.6 12.9 %collective-permute-start.11 = (f32[2,256,128]{2,1,0:T(8,128)S(1)}, f32[2,256,128]{2,1,0:T(8,128)S(1)}, u32[]{:S(2)}, u32[]{:S(2)}) collective-permute-start(f32[2,256,128]{2,1,0:T(8,128)S(1)} %get-tuple-element.65), channel_id=1, source_target_pairs={{0,4},{4,0},{8,12},{12,8},{16,20},{20,16},{24,28},{28,24},{1,5},{5... | collective-permute-start | bytes 786440 | tf_op jit(solution)/shard_map/ppermute | solution.py:354
  39.1 10.3 %collective-permute-start.12 = (f32[2,256,128]{2,1,0:T(8,128)S(1)}, f32[2,256,128]{2,1,0:T(8,128)S(1)}, u32[]{:S(2)}, u32[]{:S(2)}) collective-permute-start(f32[2,256,128]{2,1,0:T(8,128)S(1)} %get-tuple-element.66), channel_id=1, source_target_pairs={{4,8},{8,4},{12,16},{16,12},{20,24},{24,20},{5,9},{9,5},{13,17},{1... | collective-permute-start | bytes 786440 | tf_op jit(solution)/shard_map/ppermute | solution.py:354
  39.8 1.3 %collective-permute-start.9 = (f32[2,32,128]{2,1,0:T(8,128)S(1)}, f32[2,32,128]{2,1,0:T(8,128)S(1)}, u32[]{:S(2)}, u32[]{:S(2)}) collective-permute-start(f32[2,32,128]{2,1,0:T(8,128)S(1)} %get-tuple-element.59), channel_id=1, source_target_pairs={{0,1},{1,0},{2,3},{3,2},{4,5},{5,4},{6,7},{7,6},{8,9},{9,8},{10,11... | collective-permute-start | bytes 98312 | tf_op jit(solution)/shard_map/ppermute | solution.py:354
  41.1 4.8 %collective-permute-start.10 = (f32[2,32,128]{2,1,0:T(8,128)S(1)}, f32[2,32,128]{2,1,0:T(8,128)S(1)}, u32[]{:S(2)}, u32[]{:S(2)}) collective-permute-start(f32[2,32,128]{2,1,0:T(8,128)S(1)} %collective-permute-done.9.got_a), channel_id=1, source_target_pairs={{0,2},{3,1},{2,0},{1,3},{4,6},{7,5},{6,4},{5,7},{8,10},{11,9},{10,... | collective-permute-start | bytes 98312 | tf_op jit(solution)/shard_map/ppermute | solution.py:354
